TPU v7x, 256 devices: a whole 4x4x8 slice. The times are simulated.
256 devices in a mesh: expert: 16 (over y, x), tensor: 16 (over z, core).
Axes of the slice: x: 4, y: 4, z: 8, core: 2. Of those that a mesh axis runs over, the one named last changes fastest.
Arguments:
- queries: bfloat16 [4096, 8192], P('expert', 'tensor'), may hold values from -8 to 8
- keys_values: bfloat16 [16, 4, 1280, 256], P('expert'), may hold values from -6 to 6
- prefix_len: int32 [16], P('expert'), may hold values from 128 to 1024, as said below
- out_proj: bfloat16 [8192, 4096], P('tensor', 'expert'), may hold values from -0.0625 to 0.0625
- residual: bfloat16 [4096, 4096], P(('expert', 'tensor')), may hold values from -1.796875 to 1.796875
- norm_gain: float32 [4096], replicated, may hold values from 0.1 to 1.9
- expert_ids: int32 [4096, 8], P('expert'), may hold values from 0 to 63, all different within a row; in each aligned block of 16 rows (0 to 15, 16 to 31, ...) at most 3 rows name the same one
- route_weights: bfloat16 [4096, 8], P('expert'), may hold values from 0.19921875 to 1
- w_gate: bfloat16 [256, 4096, 384], P(('expert', 'tensor')), may hold values from -0.09375 to 0.09375
- w_up: bfloat16 [256, 4096, 384], P(('expert', 'tensor')), may hold values from -0.09375 to 0.09375
- w_down: bfloat16 [256, 384, 4096], P(('expert', 'tensor')), may hold values from -0.15625 to 0.15625
Outputs:
- layer_out: bfloat16 [4096, 4096], P(('expert', 'tensor'))
Inputs may be any that keep to these rules, and one draw needn't show every extreme that they name: `expert_ids`: in the rows of one device (aligned blocks of 16 rows) no expert is named by more than 3 rows, a bound that some block reaches; a row names 8 different experts. `prefix_len`: some sequence has all 1024 slots live.
All inputs are finite; a program needn't handle non-finite values.
Results may differ from a plain program's by a relative error of at most 0.035.
Values may be sent and summed in bfloat16 or wider, within the bound.
No kernel may reach another device: no remote copies, remote signals or barrier semaphores. Data moves between devices by JAX's collectives and lax.ppermute only.
A program may use at most 128 MiB of HBM per device.

v0:
```python
import math
import jax
import jax.numpy as jnp
from jax import lax
from jax.sharding import PartitionSpec as P

HEADS = 64
KVH = 4
HD = 128
TOPK = 8
HSPLIT = 4
TOK_DEV = 16
PREFIX = 1024


def norm_rows(hidden_state, norm_gain):
    values = hidden_state.astype(jnp.float32)
    factor = lax.rsqrt(jnp.mean(values * values, axis=-1, keepdims=True) + 1e-06)
    return (values * factor * norm_gain[None, :]).astype(jnp.bfloat16)


def route_tables(expert_ids, route_weights, experts, most_rows):
    total_rows = expert_ids.shape[0]
    named_mask = expert_ids[:, :, None] == jnp.arange(experts, dtype=jnp.int32)[None, None, :]
    hit_table = jnp.sum(named_mask.astype(jnp.int32), axis=1)
    weight_table = jnp.sum(
        jnp.where(named_mask, route_weights[:, :, None].astype(jnp.float32), 0.0), axis=1
    )
    grouped = hit_table.reshape(total_rows // TOK_DEV, TOK_DEV, experts)
    rank_table = (jnp.cumsum(grouped, axis=1) - grouped).reshape(total_rows, experts)
    share_index = (jnp.arange(total_rows, dtype=jnp.int32) // TOK_DEV)[:, None]
    position_table = share_index * most_rows + rank_table
    return (hit_table, weight_table, rank_table, position_table)


def pick_slot(table, expert_count, slot_count, slot_index):
    shaped = table.reshape(table.shape[0], expert_count, slot_count)
    return lax.dynamic_index_in_dim(shaped, slot_index, 2, keepdims=False)


def shards(
    queries,
    keys_values,
    prefix_len,
    out_proj,
    residual,
    norm_gain,
    expert_ids,
    route_weights,
    w_gate,
    w_up,
    w_down,
):
    tensor_count = lax.axis_size("tensor")
    expert_count = lax.axis_size("expert")
    tensor_index = lax.axis_index("tensor")
    step_rows = queries.shape[0]
    per_device = queries.shape[1] // HD
    group_size = HEADS // KVH
    kv_index = tensor_index * per_device // group_size
    cached = lax.dynamic_index_in_dim(keys_values[0], kv_index, 0, keepdims=False)
    key_rows = cached[:, :HD]
    value_rows = cached[:, HD:]
    context = cached.shape[0]
    query_rows = queries.reshape(step_rows, per_device, HD)
    scores = jnp.einsum(
        "nhd,cd->hnc", query_rows, key_rows, preferred_element_type=jnp.float32
    ) / math.sqrt(HD)
    columns = jnp.arange(context, dtype=jnp.int32)[None, :]
    positions = jnp.arange(step_rows, dtype=jnp.int32)[:, None]
    visible = ((columns < prefix_len[0]) | (columns >= PREFIX) & (columns - PREFIX <= positions))[
        None
    ]
    highest = jnp.max(jnp.where(visible, scores, -1e30), axis=-1, keepdims=True)
    weights = jnp.exp(jnp.where(visible, scores - highest, -1e30))
    summed = jnp.sum(weights, axis=-1)
    blended = jnp.einsum(
        "hnc,cd->nhd", weights.astype(jnp.bfloat16), value_rows, preferred_element_type=jnp.float32
    )
    attended = (
        (blended / jnp.transpose(summed)[:, :, None])
        .astype(jnp.bfloat16)
        .reshape(step_rows, per_device * HD)
    )
    head_part = jnp.dot(
        attended,
        lax.all_gather(out_proj, "expert", axis=1, tiled=True),
        preferred_element_type=jnp.float32,
    )
    slot_count = tensor_count // HSPLIT
    experts = expert_count * slot_count
    most_rows = min(TOK_DEV, max(2, TOK_DEV * TOPK // experts + 1))
    capacity = tensor_count * most_rows
    slot_index = tensor_index // HSPLIT
    start_row = tensor_index * TOK_DEV
    hit_table, weight_table, rank_table, position_table = route_tables(
        expert_ids, route_weights, experts, most_rows
    )
    hit_slot = pick_slot(hit_table, expert_count, slot_count, slot_index)
    weight_slot = pick_slot(weight_table, expert_count, slot_count, slot_index)
    position_slot = pick_slot(position_table, expert_count, slot_count, slot_index)
    slot_match = (hit_slot[:, :, None] == 1) & (
        position_slot[:, :, None] == jnp.arange(capacity, dtype=jnp.int32)[None, None, :]
    )
    head_sum = lax.psum(head_part.astype(jnp.bfloat16), "tensor").astype(jnp.float32)
    residual_full = lax.all_gather(residual, "tensor", axis=0, tiled=True)
    state_full = (residual_full.astype(jnp.float32) + head_sum).astype(jnp.bfloat16)
    hidden_state = lax.dynamic_slice_in_dim(state_full, start_row, TOK_DEV, 0)
    normed_full = norm_rows(state_full, norm_gain)
    source_rows = jnp.sum(
        jnp.where(slot_match, jnp.arange(step_rows, dtype=jnp.int32)[:, None, None], 0), axis=0
    )
    filled = jnp.any(slot_match, axis=0)
    outgoing = jnp.where(
        filled[:, :, None], jnp.take(normed_full, source_rows, axis=0), jnp.zeros((), jnp.bfloat16)
    )
    arrived_rows = lax.all_to_all(outgoing, "expert", split_axis=0, concat_axis=0, tiled=True)
    flat_rows = arrived_rows.reshape(-1, arrived_rows.shape[-1])
    gate_val = jnp.dot(flat_rows, w_gate[0], preferred_element_type=jnp.float32)
    up_val = jnp.dot(flat_rows, w_up[0], preferred_element_type=jnp.float32)
    inner = (jax.nn.silu(gate_val) * up_val).astype(jnp.bfloat16)
    result = jnp.dot(inner, w_down[0], preferred_element_type=jnp.float32).astype(jnp.bfloat16)
    computed = result.reshape(arrived_rows.shape)
    returned = lax.all_to_all(computed, "expert", split_axis=0, concat_axis=0, tiled=True)
    combine_weights = jnp.where(slot_match, weight_slot[:, :, None], 0.0).astype(jnp.bfloat16)
    expert_part = jnp.einsum(
        "njc,jcd->nd", combine_weights, returned, preferred_element_type=jnp.float32
    )
    expert_share = lax.psum_scatter(
        expert_part.astype(jnp.bfloat16), "tensor", scatter_dimension=0, tiled=True
    ).astype(jnp.float32)
    return (hidden_state.astype(jnp.float32) + expert_share).astype(jnp.bfloat16)


def solution(mesh):
    return jax.shard_map(
        shards,
        mesh=mesh,
        in_specs=(
            P("expert", "tensor"),
            P("expert", None, None, None),
            P("expert"),
            P("tensor", "expert"),
            P(("expert", "tensor"), None),
            P(),
            P("expert", None),
            P("expert", None),
            P(("expert", "tensor"), None, None),
            P(("expert", "tensor"), None, None),
            P(("expert", "tensor"), None, None),
        ),
        out_specs=P(("expert", "tensor"), None),
        check_vma=False,
    )
```

profile of v0, /device:TPU:2, one launch (start us, length us, event | category | flops | bytes accessed | tf_op | source)
XLA Modules:
  0.0 520.2 jit_solution(15658658182001831944)
XLA Ops:
  6.5 0.0 copy-start
  6.5 0.0 all-gather.5.cloned.1.call-start
  6.5 0.7 all-gather.5.cloned.1.call-update
  7.3 0.0 all-gather.3.cloned.1.call-start
  7.3 0.7 all-gather.3.cloned.1.call-update
  8.0 0.0 all-reduce.2.cloned.1.call-start
  8.1 0.8 convert_reduce_fusion
  8.9 0.1 copy.36
  9.7 1.1 copy.38
  10.7 1.9 reduce_window_sum.14
  12.7 2.0 dynamic-slice_bitcast_fusion
  14.7 1.0 fusion.26
  15.7 5.1 fusion.62
  20.8 2.4 fusion.33
  23.2 51.8 %all-gather.5.cloned.1.call-done = bf16[512,4096]{1,0:T(8,128)(2,1)} async-done(((bf16[512,256]{1,0:T(8,128)(2,1)}), bf16[512,4096]{1,0:T(8,128)(2,1)}) %all-gather.5.cloned.1.call-update) | async-done | bytes 4194320 | tf_op jit(solution)/shard_map/all_gather | solution.py:87
  75.0 4.8 convolution_convert_fusion.1
  79.8 0.0 all-reduce.2.cloned.1.call-update
  79.8 0.9 fusion.57
  80.8 0.4 select_reduce_fusion
  81.2 0.1 reshape.155
  81.2 0.4 fusion.37
  81.6 34.7 %all-gather.3.cloned.1.call-done = bf16[256,4096]{1,0:T(8,128)(2,1)} async-done(((bf16[16,4096]{1,0:T(8,128)(2,1)}), bf16[256,4096]{1,0:T(8,128)(2,1)}) %all-gather.3.cloned.1.call-update) | async-done | bytes 2097168 | tf_op jit(solution)/shard_map/all_gather | solution.py:106
  116.4 115.7 %all-reduce.2.cloned.1.call-done = bf16[256,4096]{1,0:T(8,128)(2,1)} async-done(((bf16[256,4096]{1,0:T(8,128)(2,1)}), bf16[256,4096]{1,0:T(8,128)(2,1)}) %all-reduce.2.cloned.1.call-update) | async-done | bytes 2097168 | tf_op jit(solution)/shard_map/psum | solution.py:105
  232.1 3.2 fusion.6
  235.2 0.0 copy-start.1
  235.3 1.3 copy-done.1
  236.6 0.0 copy-done.3
  236.6 2.0 fusion.8
  238.6 13.8 %gather_fusion = bf16[768,4096]{1,0:T(8,128)(2,1)} fusion(bf16[256,4096]{1,0:T(8,128)(2,1)} %fusion.8, s32[1024]{0:T(1024)S(1)} %pad_clamp_fusion), kind=kCustom, calls=%fused_computation | custom fusion | bytes 12585984 | tf_op jit(solution)/shard_map/jit(_take)/gather | solution.py:115
  252.4 3.9 select_select_fusion
  256.3 0.0 copy-start.5
  256.3 79.0 %all_to_all.10 = bf16[16,48,4096]{2,1,0:T(8,128)(2,1)S(1)} all-to-all(bf16[16,48,4096]{2,1,0:T(8,128)(2,1)S(1)} %select_select_fusion), channel_id=1, replica_groups=mesh['expert'=16,'tensor'=16] {'expert'}, dimensions={0} | all-to-all | bytes 12582912 | tf_op jit(solution)/shard_map/all_to_all | solution.py:117
  335.3 0.0 copy-done.5
  335.3 3.4 fusion.12
  338.7 0.0 copy-done.6
  338.7 3.5 fusion.22
  342.2 0.0 copy-done
  342.2 5.4 %convolution_convert_fusion = bf16[768,4096]{1,0:T(8,128)(2,1)} fusion(bf16[768,384]{1,0:T(8,128)(2,1)S(1)} %fusion.22, bf16[1,384,4096]{2,1,0:T(8,128)(2,1)S(1)} %copy-done), kind=kOutput, calls=%fused_computation.2 | convolution fusion | flops 2419064832 | bytes 10027008 | tf_op jit(solution)/shard_map/dot_general | solution.py:122
  347.6 6.0 %all-to-all-start.1 = ((bf16[16,48,4096]{2,1,0:T(8,128)(2,1)}), bf16[16,48,4096]{2,1,0:T(8,128)(2,1)}, u32[]{:S(2)}, u32[]{:S(2)}) async-start(bf16[16,48,4096]{2,1,0:T(8,128)(2,1)} %bitcast.108), calls=%async_computation.1 | async-start | bytes 12582912 | tf_op jit(solution)/shard_map/all_to_all | solution.py:124
  353.6 0.0 reduce-scatter.2.cloned.1.call-start
  353.6 0.0 copy-done.4
  353.7 0.0 copy-done.2
  353.7 0.1 select_reduce_fusion.1
  353.8 87.2 %all-to-all-done.1 = bf16[16,48,4096]{2,1,0:T(8,128)(2,1)} async-done(((bf16[16,48,4096]{2,1,0:T(8,128)(2,1)}), bf16[16,48,4096]{2,1,0:T(8,128)(2,1)}, u32[]{:S(2)}, u32[]{:S(2)}) %all-to-all-start.1) | async-done | bytes 6291488 | tf_op jit(solution)/shard_map/all_to_all | solution.py:124
  441.0 6.0 %fusion.3 = bf16[256,4096]{1,0:T(8,128)(2,1)} fusion(bf16[16,48,4096]{2,1,0:T(8,128)(2,1)} %all-to-all-done.1, bf16[256,16]{0,1:T(8,128)(2,1)S(1)} %bitcast.119, s32[256,16]{0,1:T(8,128)S(1)} %bitcast.113, pred[256,16]{0,1:T(8,128)(4,1)S(1)} %bitcast.118), kind=kOutput, calls=%fused_computation.11 | convolution fusion | flops 1612251136 | bytes 8417280 | tf_op jit(solution)/shard_map/njc,jcd->nd/dot_general | solution.py:126
  447.0 0.0 reduce-scatter.2.cloned.1.call-update
  447.0 65.0 %reduce-scatter.2.cloned.1.call-done = bf16[16,4096]{1,0:T(8,128)(2,1)} async-done(((bf16[256,4096]{1,0:T(8,128)(2,1)}), bf16[16,4096]{1,0:T(8,128)(2,1)}) %reduce-scatter.2.cloned.1.call-update) | async-done | bytes 131088 | tf_op jit(solution)/shard_map/reduce_scatter | solution.py:129
  512.0 1.7 add_convert_fusion.1
  (20 shorter events, 0.2 us)
Async XLA Ops:
  6.5 335.7 %copy-start = (bf16[1,384,4096]{2,1,0:T(8,128)(2,1)S(1)}, bf16[1,384,4096]{2,1,0:T(8,128)(2,1)}, u32[]{:S(2)}) copy-start(bf16[1,384,4096]{2,1,0:T(8,128)(2,1)} %param.21) | copy-start | bytes 9437188
  6.5 68.5 %all-gather.5.cloned.1.call-start = ((), (), s32[]{:S(2)}) async-start(), calls=%async_computation.4 | async-start | bytes 4456448 | tf_op jit(solution)/shard_map/all_gather | solution.py:87
  7.3 109.1 %all-gather.3.cloned.1.call-start = ((), (), s32[]{:S(2)}) async-start(), calls=%async_computation.3 | async-start | bytes 2228224 | tf_op jit(solution)/shard_map/all_gather | solution.py:106
  8.0 224.1 %all-reduce.2.cloned.1.call-start = ((), (), s32[]{:S(2)}) async-start(), calls=%async_computation.5 | async-start | bytes 4194304 | tf_op jit(solution)/shard_map/psum | solution.py:105
  79.8 156.8 %copy-start.3 = (f32[4096]{0:T(1024)S(1)}, f32[4096]{0:T(1024)}, u32[]{:S(2)}) copy-start(f32[4096]{0:T(1024)} %param.16) | copy-start | bytes 49156
  235.2 1.4 copy-start.1
  256.3 79.0 %copy-start.5 = (bf16[1,4096,384]{2,1,0:T(8,128)(2,1)S(1)}, bf16[1,4096,384]{2,1,0:T(8,128)(2,1)}, u32[]{:S(2)}) copy-start(bf16[1,4096,384]{2,1,0:T(8,128)(2,1)} %param.19) | copy-start | bytes 9437188
  335.3 3.4 copy-start.6
  347.6 6.0 %copy-start.4 = (bf16[256,8]{0,1:T(8,128)(2,1)S(1)}, bf16[256,8]{0,1:T(8,128)(2,1)}, u32[]{:S(2)}) copy-start(bf16[256,8]{0,1:T(8,128)(2,1)} %param.18) | copy-start | bytes 12292
  347.6 6.0 %copy-start.2 = (s32[256,8]{0,1:T(8,128)S(1)}, s32[256,8]{0,1:T(8,128)}, u32[]{:S(2)}) copy-start(s32[256,8]{0,1:T(8,128)} %param.17) | copy-start | bytes 24580
  347.6 93.4 %all-to-all-start.1 = ((bf16[16,48,4096]{2,1,0:T(8,128)(2,1)}), bf16[16,48,4096]{2,1,0:T(8,128)(2,1)}, u32[]{:S(2)}, u32[]{:S(2)}) async-start(bf16[16,48,4096]{2,1,0:T(8,128)(2,1)} %bitcast.108), calls=%async_computation.1 | async-start | bytes 12582912 | tf_op jit(solution)/shard_map/all_to_all | solution.py:124
  353.6 158.4 %reduce-scatter.2.cloned.1.call-start = ((), (), s32[]{:S(2)}) async-start(), calls=%async_computation.6 | async-start | bytes 2228224 | tf_op jit(solution)/shard_map/reduce_scatter | solution.py:129
Sparse Core Ops, SparseCore 0:
  9.8 65.2 all-gather.4
  76.8 39.4 all-gather.2
  118.7 113.3 all-reduce.1
  447.2 64.7 reduce-scatter.1
where the time goes:
time: 521 us; the launch traced here: 520 us
  waiting for transfers between devices  356 us (68%)
  blocking collectives  79 us (15%)
  matrix products  30.6 us (6%)
  local copies, waits for them, and re-layouts  20.5 us (4%)
  other arithmetic  14.3 us (3%)
  between operations  14 us (3%)
  starting transfers between devices  6.07 us (1%)
    psum x1, waiting for transfers between devices, shards(): lax.psum(head_part.astype(jnp.bfloat16), 'tensor').astype(jnp.float32)  116 us
    all_to_all x1, waiting for transfers between devices, shards(): lax.all_to_all(computed, 'expert', split_axis=0, concat_axis=0, tiled=True)  87.2 us
    all_to_all x1, blocking collectives, shards(): lax.all_to_all(outgoing, 'expert', split_axis=0, concat_axis=0, tiled=True)  79 us
    reduce_scatter x1, waiting for transfers between devices, shards(): lax.psum_scatter(expert_part.astype(jnp.bfloat16), 'tensor', scatter_dime...  65 us
    all_gather x1, waiting for transfers between devices, shards(): lax.all_gather(out_proj, 'expert', axis=1, tiled=True)  51.8 us
    all_gather x1, waiting for transfers between devices, shards(): residual_full = lax.all_gather(residual, 'tensor', axis=0, tiled=True)  34.7 us
    gather x1, local copies, waits for them, and re-layouts, shards(): jnp.take(normed_full, source_rows, axis=0)  13.8 us
  transfers between devices with their start and end apart: 5, of which 5 were waited for; matrix products, arithmetic and copies ran while one was open for 4% of the time, Pallas kernels for 0%

commit v1 on v0

--- a/solution.py
+++ b/solution.py
@@ -11,6 +11,27 @@
 HSPLIT = 4
 TOK_DEV = 16
 PREFIX = 1024
+
+
+def collect(shard, axis, dim):
+    size, position, rows = (lax.axis_size(axis), lax.axis_index(axis), shard.shape[dim])
+    right = [(i, (i + 1) % size) for i in range(size)]
+    left = [(i, (i - 1) % size) for i in range(size)]
+    filled = jnp.zeros((*shard.shape[:dim], size * rows, *shard.shape[dim + 1 :]), shard.dtype)
+    filled = lax.dynamic_update_slice_in_dim(filled, shard, position * rows, axis=dim)
+    from_left = from_right = shard
+    halfway = size // 2
+    for step in range(1, halfway + 1):
+        from_left = lax.ppermute(from_left, axis, right)
+        filled = lax.dynamic_update_slice_in_dim(
+            filled, from_left, (position - step) % size * rows, axis=dim
+        )
+        if step < size - halfway:
+            from_right = lax.ppermute(from_right, axis, left)
+            filled = lax.dynamic_update_slice_in_dim(
+                filled, from_right, (position + step) % size * rows, axis=dim
+            )
+    return filled
 
 
 def norm_rows(hidden_state, norm_gain):
@@ -103,7 +124,7 @@
         position_slot[:, :, None] == jnp.arange(capacity, dtype=jnp.int32)[None, None, :]
     )
     head_sum = lax.psum(head_part.astype(jnp.bfloat16), "tensor").astype(jnp.float32)
-    residual_full = lax.all_gather(residual, "tensor", axis=0, tiled=True)
+    residual_full = collect(residual, "tensor", 0)
     state_full = (residual_full.astype(jnp.float32) + head_sum).astype(jnp.bfloat16)
     hidden_state = lax.dynamic_slice_in_dim(state_full, start_row, TOK_DEV, 0)
     normed_full = norm_rows(state_full, norm_gain)

time: 521 us -> 484 us (0.929)
  waiting for transfers between devices: 356 us -> 279 us
  starting transfers between devices: 6.07 us -> 29.2 us
  local copies, waits for them, and re-layouts: 20.5 us -> 37.3 us
    all_gather x1, waiting for transfers between devices: 51.8 us -> 10.8 us  [shards(): lax.all_gather(out_proj, 'expert', axis=1, tiled=True)]
    all_gather x1 -> x0, waiting for transfers between devices: 34.7 us -> none  [shards(): residual_full = lax.all_gather(residual, 'tensor', axis=0, tiled=True)]
    ppermute x0 -> x15, starting transfers between devices: none -> 23.2 us  [the longest x7 23.1 us: collect(): from_right = lax.ppermute(from_right, axis, left)]
    dynamic_update_slice x0 -> x16, local copies, waits for them, and re-layouts: none -> 15.9 us  [the longest x8 7.96 us: collect(): lax.dynamic_update_slice_in_dim(filled, from_left, (position - step) % si...]
    ppermute x0 -> x15, waiting for transfers between devices: none -> 5.74 us  [the longest x8 5.72 us: collect(): from_left = lax.ppermute(from_left, axis, right)]
    psum x1, waiting for transfers between devices: 116 us -> 110 us  [shards(): lax.psum(head_part.astype(jnp.bfloat16), 'tensor').astype(jnp.float32)]
  transfers between devices with their start and end apart: 5 -> 19, of which waited for: 5 -> 9; matrix products, arithmetic and copies ran while one was open for 4% -> 8% of each run, Pallas kernels for 0% -> 0%
where the time goes in v1:
time: 484 us; the launch traced here: 483 us
  waiting for transfers between devices  279 us (58%)
  blocking collectives  79 us (16%)
  local copies, waits for them, and re-layouts  37.3 us (8%)
  matrix products  30.7 us (6%)
  starting transfers between devices  29.2 us (6%)
  between operations  14.3 us (3%)
  other arithmetic  13.4 us (3%)
    psum x1, waiting for transfers between devices, shards(): lax.psum(head_part.astype(jnp.bfloat16), 'tensor').astype(jnp.float32)  110 us
    all_to_all x1, waiting for transfers between devices, shards(): lax.all_to_all(computed, 'expert', split_axis=0, concat_axis=0, tiled=True)  87.2 us
    all_to_all x1, blocking collectives, shards(): lax.all_to_all(outgoing, 'expert', split_axis=0, concat_axis=0, tiled=True)  79 us
    reduce_scatter x1, waiting for transfers between devices, shards(): lax.psum_scatter(expert_part.astype(jnp.bfloat16), 'tensor', scatter_dime...  65 us
    ppermute x7, starting transfers between devices, collect(): from_right = lax.ppermute(from_right, axis, left)  23.1 us
    gather x1, local copies, waits for them, and re-layouts, shards(): jnp.take(normed_full, source_rows, axis=0)  13.8 us
    all_gather x1, waiting for transfers between devices, shards(): lax.all_gather(out_proj, 'expert', axis=1, tiled=True)  10.8 us
  transfers between devices with their start and end apart: 19, of which 9 were waited for; matrix products, arithmetic and copies ran while one was open for 8% of the time, Pallas kernels for 0%

profile of v1, /device:TPU:2, one launch (start us, length us, event | category | flops | bytes accessed | tf_op | source)
XLA Modules:
  0.0 482.9 jit_solution(11917246560910012783)
XLA Ops:
  6.5 5.3 %collective-permute-start.1 = (bf16[16,4096]{1,0:T(8,128)(2,1)}, bf16[16,4096]{1,0:T(8,128)(2,1)}, u32[]{:S(2)}, u32[]{:S(2)}) collective-permute-start(bf16[16,4096]{1,0:T(8,128)(2,1)} %param.15), channel_id=1, source_target_pairs={{0,15},{1,0},{2,1},{3,2},{4,3},{5,4},{6,5},{7,6},{8,7},{9,8},{10,9... | collective-permute-start | bytes 393224 | tf_op jit(solution)/shard_map/ppermute | solution.py:30
  11.9 0.8 convert_reduce_fusion
  13.6 1.1 copy.38
  14.6 1.3 reduce_window_sum.14
  16.7 2.0 dynamic-slice_bitcast_fusion
  18.7 1.0 fusion.26
  19.7 5.1 %fusion.62 = (f32[4,256]{1,0:T(4,128)S(1)}, bf16[4,256,1280]{1,2,0:T(8,128)(2,1)}) fusion(pred[256,1280]{0,1:T(8,128)(4,1)S(1)} %fusion.26, bf16[1280,256]{1,0:T(8,128)(2,1)} %dynamic-slice_bitcast_fusion, bf16[256,512]{1,0:T(8,128)(2,1)} %param.11), kind=kOutput, calls=%fused_computation.100 | convolution fusion | flops 680264960 | bytes 4460544 | tf_op jit(solution)/shard_map/sub | solution.py:96
  24.8 2.5 fusion.33
  27.4 1.6 broadcast_in_dim.96
  29.0 0.7 constant_dynamic-update-slice_fusion.15
  30.0 2.9 collective-permute-start.3
  33.0 1.6 constant_dynamic-update-slice_fusion.14
  34.5 1.6 constant_dynamic-update-slice_fusion.13
  36.1 3.0 collective-permute-start.5
  39.1 0.7 constant_dynamic-update-slice_fusion.12
  39.7 0.7 constant_dynamic-update-slice_fusion.11
  40.4 1.3 collective-permute-done.4
  41.7 3.0 collective-permute-start.7
  45.3 0.7 constant_dynamic-update-slice_fusion.9
  46.0 1.3 collective-permute-done.6
  47.3 3.0 collective-permute-start.9
  50.3 0.7 constant_dynamic-update-slice_fusion.8
  50.9 0.7 constant_dynamic-update-slice_fusion.7
  51.6 1.3 collective-permute-done.8
  52.9 3.0 collective-permute-start.11
  57.2 1.3 collective-permute-done.10
  58.5 3.1 collective-permute-start.13
  62.3 1.6 constant_dynamic-update-slice_fusion.3
  64.2 10.8 %all-gather.2.cloned.1.call-done = bf16[512,4096]{1,0:T(8,128)(2,1)} async-done(((bf16[512,256]{1,0:T(8,128)(2,1)}), bf16[512,4096]{1,0:T(8,128)(2,1)}) %all-gather.2.cloned.1.call-update) | async-done | bytes 4194320 | tf_op jit(solution)/shard_map/all_gather | solution.py:108
  75.0 4.8 convolution_convert_fusion.1
  79.8 1.6 constant_dynamic-update-slice_fusion.2
  81.4 1.6 constant_dynamic-update-slice_fusion.1
  83.0 1.6 constant_dynamic-update-slice_fusion
  84.5 110.2 %all-reduce.2.cloned.1.call-done = bf16[256,4096]{1,0:T(8,128)(2,1)} async-done(((bf16[256,4096]{1,0:T(8,128)(2,1)}), bf16[256,4096]{1,0:T(8,128)(2,1)}) %all-reduce.2.cloned.1.call-update) | async-done | bytes 2097168 | tf_op jit(solution)/shard_map/psum | solution.py:126
  194.8 3.2 fusion.6
  198.0 1.3 copy-done.1
  199.3 2.0 fusion.8
  201.3 13.8 %gather_fusion = bf16[768,4096]{1,0:T(8,128)(2,1)} fusion(bf16[256,4096]{1,0:T(8,128)(2,1)} %fusion.8, s32[1024]{0:T(1024)S(1)} %pad_clamp_fusion), kind=kCustom, calls=%fused_computation | custom fusion | bytes 12585984 | tf_op jit(solution)/shard_map/jit(_take)/gather | solution.py:136
  215.1 3.9 select_select_fusion
  219.0 79.0 %all_to_all.10 = bf16[16,48,4096]{2,1,0:T(8,128)(2,1)S(1)} all-to-all(bf16[16,48,4096]{2,1,0:T(8,128)(2,1)S(1)} %select_select_fusion), channel_id=1, replica_groups=mesh['expert'=16,'tensor'=16] {'expert'}, dimensions={0} | all-to-all | bytes 12582912 | tf_op jit(solution)/shard_map/all_to_all | solution.py:138
  298.0 3.4 fusion.12
  301.4 3.5 fusion.22
  304.9 5.4 %convolution_convert_fusion = bf16[768,4096]{1,0:T(8,128)(2,1)} fusion(bf16[768,384]{1,0:T(8,128)(2,1)S(1)} %fusion.22, bf16[1,384,4096]{2,1,0:T(8,128)(2,1)S(1)} %copy-done), kind=kOutput, calls=%fused_computation.2 | convolution fusion | flops 2419064832 | bytes 10027008 | tf_op jit(solution)/shard_map/dot_general | solution.py:143
  310.3 6.0 %all-to-all-start.1 = ((bf16[16,48,4096]{2,1,0:T(8,128)(2,1)}), bf16[16,48,4096]{2,1,0:T(8,128)(2,1)}, u32[]{:S(2)}, u32[]{:S(2)}) async-start(bf16[16,48,4096]{2,1,0:T(8,128)(2,1)} %bitcast.108), calls=%async_computation.1 | async-start | bytes 12582912 | tf_op jit(solution)/shard_map/all_to_all | solution.py:145
  316.5 87.2 %all-to-all-done.1 = bf16[16,48,4096]{2,1,0:T(8,128)(2,1)} async-done(((bf16[16,48,4096]{2,1,0:T(8,128)(2,1)}), bf16[16,48,4096]{2,1,0:T(8,128)(2,1)}, u32[]{:S(2)}, u32[]{:S(2)}) %all-to-all-start.1) | async-done | bytes 6291488 | tf_op jit(solution)/shard_map/all_to_all | solution.py:145
  403.7 6.0 %fusion.3 = bf16[256,4096]{1,0:T(8,128)(2,1)} fusion(bf16[16,48,4096]{2,1,0:T(8,128)(2,1)} %all-to-all-done.1, bf16[256,16]{0,1:T(8,128)(2,1)S(1)} %bitcast.119, s32[256,16]{0,1:T(8,128)S(1)} %bitcast.113, pred[256,16]{0,1:T(8,128)(4,1)S(1)} %bitcast.118), kind=kOutput, calls=%fused_computation.11 | convolution fusion | flops 1612251136 | bytes 8417280 | tf_op jit(solution)/shard_map/njc,jcd->nd/dot_general | solution.py:147
  409.7 65.0 %reduce-scatter.2.cloned.1.call-done = bf16[16,4096]{1,0:T(8,128)(2,1)} async-done(((bf16[256,4096]{1,0:T(8,128)(2,1)}), bf16[16,4096]{1,0:T(8,128)(2,1)}) %reduce-scatter.2.cloned.1.call-update) | async-done | bytes 131088 | tf_op jit(solution)/shard_map/reduce_scatter | solution.py:150
  474.7 1.7 add_convert_fusion.1
  (66 shorter events, 4.4 us)
Async XLA Ops:
  6.5 298.3 %copy-start = (bf16[1,384,4096]{2,1,0:T(8,128)(2,1)S(1)}, bf16[1,384,4096]{2,1,0:T(8,128)(2,1)}, u32[]{:S(2)}) copy-start(bf16[1,384,4096]{2,1,0:T(8,128)(2,1)} %param.21) | copy-start | bytes 9437188
  6.5 68.5 %all-gather.2.cloned.1.call-start = ((), (), s32[]{:S(2)}) async-start(), calls=%async_computation.3 | async-start | bytes 4456448 | tf_op jit(solution)/shard_map/all_gather | solution.py:108
  6.5 23.4 %collective-permute-start = (bf16[16,4096]{1,0:T(8,128)(2,1)}, bf16[16,4096]{1,0:T(8,128)(2,1)}, u32[]{:S(2)}, u32[]{:S(2)}) collective-permute-start(bf16[16,4096]{1,0:T(8,128)(2,1)} %param.15), channel_id=1, source_target_pairs={{0,1},{1,2},{2,3},{3,4},{4,5},{5,6},{6,7},{7,8},{8,9},{9,10},{10,1... | collective-permute-start | bytes 393224 | tf_op jit(solution)/shard_map/ppermute | solution.py:25
  6.5 23.5 %collective-permute-start.1 = (bf16[16,4096]{1,0:T(8,128)(2,1)}, bf16[16,4096]{1,0:T(8,128)(2,1)}, u32[]{:S(2)}, u32[]{:S(2)}) collective-permute-start(bf16[16,4096]{1,0:T(8,128)(2,1)} %param.15), channel_id=1, source_target_pairs={{0,15},{1,0},{2,1},{3,2},{4,3},{5,4},{6,5},{7,6},{8,7},{9,8},{10,9... | collective-permute-start | bytes 393224 | tf_op jit(solution)/shard_map/ppermute | solution.py:30
  11.9 182.9 %all-reduce.2.cloned.1.call-start = ((), (), s32[]{:S(2)}) async-start(), calls=%async_computation.4 | async-start | bytes 4194304 | tf_op jit(solution)/shard_map/psum | solution.py:126
  24.8 4.1 copy-start.2
  30.0 6.1 %collective-permute-start.2 = (bf16[16,4096]{1,0:T(8,128)(2,1)}, bf16[16,4096]{1,0:T(8,128)(2,1)S(1)}, u32[]{:S(2)}, u32[]{:S(2)}) collective-permute-start(bf16[16,4096]{1,0:T(8,128)(2,1)} %collective-permute-done), channel_id=1, source_target_pairs={{0,1},{1,2},{2,3},{3,4},{4,5},{5,6},{6,7},{7,8},{8,9},{9,10},{10,1... | collective-permute-start | bytes 393224 | tf_op jit(solution)/shard_map/ppermute | solution.py:25
  30.0 6.1 %collective-permute-start.3 = (bf16[16,4096]{1,0:T(8,128)(2,1)}, bf16[16,4096]{1,0:T(8,128)(2,1)S(1)}, u32[]{:S(2)}, u32[]{:S(2)}) collective-permute-start(bf16[16,4096]{1,0:T(8,128)(2,1)} %collective-permute-done.1), channel_id=1, source_target_pairs={{0,15},{1,0},{2,1},{3,2},{4,3},{5,4},{6,5},{7,6},{8,7},{9,8},{10,9... | collective-permute-start | bytes 393224 | tf_op jit(solution)/shard_map/ppermute | solution.py:30
  36.1 5.6 %collective-permute-start.4 = (bf16[16,4096]{1,0:T(8,128)(2,1)S(1)}, bf16[16,4096]{1,0:T(8,128)(2,1)S(1)}, u32[]{:S(2)}, u32[]{:S(2)}) collective-permute-start(bf16[16,4096]{1,0:T(8,128)(2,1)S(1)} %collective-permute-done.2), channel_id=1, source_target_pairs={{0,1},{1,2},{2,3},{3,4},{4,5},{5,6},{6,7},{7,8},{8,9},{9,10},{10,1... | collective-permute-start | bytes 393224 | tf_op jit(solution)/shard_map/ppermute | solution.py:25
  36.1 5.6 %collective-permute-start.5 = (bf16[16,4096]{1,0:T(8,128)(2,1)S(1)}, bf16[16,4096]{1,0:T(8,128)(2,1)S(1)}, u32[]{:S(2)}, u32[]{:S(2)}) collective-permute-start(bf16[16,4096]{1,0:T(8,128)(2,1)S(1)} %collective-permute-done.3), channel_id=1, source_target_pairs={{0,15},{1,0},{2,1},{3,2},{4,3},{5,4},{6,5},{7,6},{8,7},{9,8},{10,9... | collective-permute-start | bytes 393224 | tf_op jit(solution)/shard_map/ppermute | solution.py:30
  41.7 5.6 %collective-permute-start.6 = (bf16[16,4096]{1,0:T(8,128)(2,1)S(1)}, bf16[16,4096]{1,0:T(8,128)(2,1)S(1)}, u32[]{:S(2)}, u32[]{:S(2)}) collective-permute-start(bf16[16,4096]{1,0:T(8,128)(2,1)S(1)} %collective-permute-done.4), channel_id=1, source_target_pairs={{0,1},{1,2},{2,3},{3,4},{4,5},{5,6},{6,7},{7,8},{8,9},{9,10},{10,1... | collective-permute-start | bytes 393224 | tf_op jit(solution)/shard_map/ppermute | solution.py:25
  41.7 5.6 %collective-permute-start.7 = (bf16[16,4096]{1,0:T(8,128)(2,1)S(1)}, bf16[16,4096]{1,0:T(8,128)(2,1)S(1)}, u32[]{:S(2)}, u32[]{:S(2)}) collective-permute-start(bf16[16,4096]{1,0:T(8,128)(2,1)S(1)} %collective-permute-done.5), channel_id=1, source_target_pairs={{0,15},{1,0},{2,1},{3,2},{4,3},{5,4},{6,5},{7,6},{8,7},{9,8},{10,9... | collective-permute-start | bytes 393224 | tf_op jit(solution)/shard_map/ppermute | solution.py:30
  47.3 5.6 %collective-permute-start.8 = (bf16[16,4096]{1,0:T(8,128)(2,1)S(1)}, bf16[16,4096]{1,0:T(8,128)(2,1)S(1)}, u32[]{:S(2)}, u32[]{:S(2)}) collective-permute-start(bf16[16,4096]{1,0:T(8,128)(2,1)S(1)} %collective-permute-done.6), channel_id=1, source_target_pairs={{0,1},{1,2},{2,3},{3,4},{4,5},{5,6},{6,7},{7,8},{8,9},{9,10},{10,1... | collective-permute-start | bytes 393224 | tf_op jit(solution)/shard_map/ppermute | solution.py:25
  47.3 5.6 %collective-permute-start.9 = (bf16[16,4096]{1,0:T(8,128)(2,1)S(1)}, bf16[16,4096]{1,0:T(8,128)(2,1)S(1)}, u32[]{:S(2)}, u32[]{:S(2)}) collective-permute-start(bf16[16,4096]{1,0:T(8,128)(2,1)S(1)} %collective-permute-done.7), channel_id=1, source_target_pairs={{0,15},{1,0},{2,1},{3,2},{4,3},{5,4},{6,5},{7,6},{8,7},{9,8},{10,9... | collective-permute-start | bytes 393224 | tf_op jit(solution)/shard_map/ppermute | solution.py:30
  52.9 5.6 %collective-permute-start.10 = (bf16[16,4096]{1,0:T(8,128)(2,1)S(1)}, bf16[16,4096]{1,0:T(8,128)(2,1)S(1)}, u32[]{:S(2)}, u32[]{:S(2)}) collective-permute-start(bf16[16,4096]{1,0:T(8,128)(2,1)S(1)} %collective-permute-done.8), channel_id=1, source_target_pairs={{0,1},{1,2},{2,3},{3,4},{4,5},{5,6},{6,7},{7,8},{8,9},{9,10},{10,1... | collective-permute-start | bytes 393224 | tf_op jit(solution)/shard_map/ppermute | solution.py:25
  52.9 5.6 %collective-permute-start.11 = (bf16[16,4096]{1,0:T(8,128)(2,1)S(1)}, bf16[16,4096]{1,0:T(8,128)(2,1)}, u32[]{:S(2)}, u32[]{:S(2)}) collective-permute-start(bf16[16,4096]{1,0:T(8,128)(2,1)S(1)} %collective-permute-done.9), channel_id=1, source_target_pairs={{0,15},{1,0},{2,1},{3,2},{4,3},{5,4},{6,5},{7,6},{8,7},{9,8},{10,9... | collective-permute-start | bytes 393224 | tf_op jit(solution)/shard_map/ppermute | solution.py:30
  58.5 5.7 %collective-permute-start.12 = (bf16[16,4096]{1,0:T(8,128)(2,1)S(1)}, bf16[16,4096]{1,0:T(8,128)(2,1)}, u32[]{:S(2)}, u32[]{:S(2)}) collective-permute-start(bf16[16,4096]{1,0:T(8,128)(2,1)S(1)} %collective-permute-done.10), channel_id=1, source_target_pairs={{0,1},{1,2},{2,3},{3,4},{4,5},{5,6},{6,7},{7,8},{8,9},{9,10},{10,1... | collective-permute-start | bytes 393224 | tf_op jit(solution)/shard_map/ppermute | solution.py:25
  58.5 22.9 %collective-permute-start.13 = (bf16[16,4096]{1,0:T(8,128)(2,1)}, bf16[16,4096]{1,0:T(8,128)(2,1)}, u32[]{:S(2)}, u32[]{:S(2)}) collective-permute-start(bf16[16,4096]{1,0:T(8,128)(2,1)} %collective-permute-done.11), channel_id=1, source_target_pairs={{0,15},{1,0},{2,1},{3,2},{4,3},{5,4},{6,5},{7,6},{8,7},{9,8},{10,9... | collective-permute-start | bytes 393224 | tf_op jit(solution)/shard_map/ppermute | solution.py:30
  64.2 18.7 %collective-permute-start.14 = (bf16[16,4096]{1,0:T(8,128)(2,1)}, bf16[16,4096]{1,0:T(8,128)(2,1)}, u32[]{:S(2)}, u32[]{:S(2)}) collective-permute-start(bf16[16,4096]{1,0:T(8,128)(2,1)} %collective-permute-done.12), channel_id=1, source_target_pairs={{0,1},{1,2},{2,3},{3,4},{4,5},{5,6},{6,7},{7,8},{8,9},{9,10},{10,1... | collective-permute-start | bytes 393224 | tf_op jit(solution)/shard_map/ppermute | solution.py:25
  84.5 114.7 %copy-start.4 = (f32[4096]{0:T(1024)S(1)}, f32[4096]{0:T(1024)}, u32[]{:S(2)}) copy-start(f32[4096]{0:T(1024)} %param.16) | copy-start | bytes 49156
  197.9 1.3 copy-start.1
  219.0 79.0 %copy-start.6 = (bf16[1,4096,384]{2,1,0:T(8,128)(2,1)S(1)}, bf16[1,4096,384]{2,1,0:T(8,128)(2,1)}, u32[]{:S(2)}) copy-start(bf16[1,4096,384]{2,1,0:T(8,128)(2,1)} %param.19) | copy-start | bytes 9437188
  298.0 3.4 copy-start.7
  310.3 6.0 %copy-start.5 = (bf16[256,8]{0,1:T(8,128)(2,1)S(1)}, bf16[256,8]{0,1:T(8,128)(2,1)}, u32[]{:S(2)}) copy-start(bf16[256,8]{0,1:T(8,128)(2,1)} %param.18) | copy-start | bytes 12292
  310.3 6.0 %copy-start.3 = (s32[256,8]{0,1:T(8,128)S(1)}, s32[256,8]{0,1:T(8,128)}, u32[]{:S(2)}) copy-start(s32[256,8]{0,1:T(8,128)} %param.17) | copy-start | bytes 24580
  310.3 93.4 %all-to-all-start.1 = ((bf16[16,48,4096]{2,1,0:T(8,128)(2,1)}), bf16[16,48,4096]{2,1,0:T(8,128)(2,1)}, u32[]{:S(2)}, u32[]{:S(2)}) async-start(bf16[16,48,4096]{2,1,0:T(8,128)(2,1)} %bitcast.108), calls=%async_computation.1 | async-start | bytes 12582912 | tf_op jit(solution)/shard_map/all_to_all | solution.py:145
  316.3 158.4 %reduce-scatter.2.cloned.1.call-start = ((), (), s32[]{:S(2)}) async-start(), calls=%async_computation.5 | async-start | bytes 2228224 | tf_op jit(solution)/shard_map/reduce_scatter | solution.py:150
Sparse Core Ops, SparseCore 0:
  12.0 62.9 all-gather.1
  80.0 114.7 all-reduce.1
  409.8 64.7 reduce-scatter.1
